TPU v7x, 256 devices: a whole 4x4x8 slice. The times are simulated.
256 devices in a mesh: frame: 16 (over z_hi, y), space: 16 (over z_lo, x, core).
Axes of the slice: x: 4, y: 4, z: 8 (z_hi: 4, z_lo: 2; z = z_hi * 2 + z_lo), core: 2. Of those that a mesh axis runs over, the one named last changes fastest.
Arguments:
- hidden_in: bfloat16 [2, 16, 32, 64, 1152], P(None, 'frame', 'space'), may hold values from -6 to 6
- attn_cotangent: bfloat16 [2, 16, 32, 64, 1152], P(None, 'frame', 'space'), may hold values from -6 to 6
- w_qkv: bfloat16 [1152, 3456], P('space'), may hold values from -0.1875 to 0.1875
- modulation_table: bfloat16 [1000, 2, 1152], replicated, may hold values from -3 to 3
- snr_table: float32 [1000], replicated, may hold values from 0.1 to 1
- timestep: int32 [2], replicated, may hold values from 0 to 999
- weight_index: int32 [2], replicated, may hold values from 0 to 999
Outputs:
- grad_input: bfloat16 [2, 16, 32, 64, 1152], P(None, 'frame', 'space')
- grad_w_qkv: float32 [1152, 3456], P('space')
- grad_modulation: float32 [2, 2, 1152], replicated
All inputs are finite; a program needn't handle non-finite values.
Results may differ from a plain program's by a relative error of at most 0.029.
Values may be sent and summed in bfloat16 or wider, within the bound.
A program may use at most 128 MiB of HBM per device.

v0:
```python
import jax
import jax.numpy as jnp
from jax import lax
from jax.sharding import PartitionSpec as P

HEADS = 16
HEAD_DIM = 72


def attend_back(queries, keys, values, upstream):
    factor = queries.shape[-1] ** (-0.5)
    queries = queries.astype(jnp.float32)
    keys = keys.astype(jnp.float32)
    values = values.astype(jnp.float32)
    upstream = upstream.astype(jnp.float32)
    highest = lax.Precision.HIGHEST
    scores = jnp.einsum("bfxhe,bgxhe->bxhfg", queries, keys, precision=highest) * factor
    expd = jnp.exp(scores)
    probs = expd / jnp.sum(expd, axis=-1, keepdims=True)
    grad_probs = jnp.einsum("bfxhe,bgxhe->bxhfg", upstream, values, precision=highest)
    grad_values = jnp.einsum("bxhfg,bfxhe->bgxhe", probs, upstream, precision=highest)
    grad_scores = probs * (grad_probs - jnp.sum(probs * grad_probs, axis=-1, keepdims=True))
    grad_queries = jnp.einsum("bxhfg,bgxhe->bfxhe", grad_scores, keys, precision=highest) * factor
    grad_keys = jnp.einsum("bxhfg,bfxhe->bgxhe", grad_scores, queries, precision=highest) * factor
    return (
        grad_queries.astype(jnp.bfloat16),
        grad_keys.astype(jnp.bfloat16),
        grad_values.astype(jnp.bfloat16),
    )


def per_device(
    hidden_in, attn_cotangent, w_qkv, modulation_table, snr_table, timestep, weight_index
):
    clip_count, frame_dev, row_dev, col_count, model_width = hidden_in.shape
    positions = row_dev * col_count
    values_in = hidden_in.astype(jnp.float32)
    average = jnp.mean(values_in, axis=-1, keepdims=True)
    centered = values_in - average
    variance = jnp.mean(centered * centered, axis=-1, keepdims=True)
    inverse_std = lax.rsqrt(variance + 1e-06)
    normed = centered * inverse_std
    modulation = modulation_table[timestep].astype(jnp.float32)
    shift = modulation[:, 0][:, None, None, None, :]
    scale = modulation[:, 1][:, None, None, None, :]
    modulated = (normed * (1.0 + scale) + shift).astype(jnp.bfloat16)
    mod_rows = modulated.reshape(-1, model_width)
    w_full = lax.all_gather(w_qkv, "space", axis=0, tiled=True)
    projected = jnp.dot(mod_rows, w_full, preferred_element_type=jnp.float32).astype(jnp.bfloat16)
    projected = projected.reshape(clip_count, frame_dev, positions, 3, model_width)
    loss_weight = snr_table[weight_index]
    upstream = (loss_weight[:, None, None, None, None] * attn_cotangent.astype(jnp.float32)).astype(
        jnp.bfloat16
    )
    upstream = upstream.reshape(clip_count, frame_dev, positions, 1, model_width)
    packed = jnp.concatenate([projected, upstream], axis=3)
    received = lax.all_to_all(packed, "frame", split_axis=2, concat_axis=1, tiled=True)
    item_count = received.shape[0]
    frames = received.shape[1]
    across = received.shape[2]
    pieces = received.reshape(item_count, frames, across, 4, HEADS, HEAD_DIM)
    head_grads = attend_back(
        pieces[:, :, :, 0], pieces[:, :, :, 1], pieces[:, :, :, 2], pieces[:, :, :, 3]
    )
    stacked = jnp.stack(head_grads, axis=3).reshape(item_count, frames, across, 3, model_width)
    grad_projected = lax.all_to_all(stacked, "frame", split_axis=1, concat_axis=2, tiled=True)
    grad_rows = grad_projected.reshape(-1, 3 * model_width)
    device_count = lax.axis_size("frame") * lax.axis_size("space")
    grad_scale_factor = float(mod_rows.shape[0] * device_count) ** (-0.5)
    row_share = lax.psum_scatter(
        lax.dot_general(
            mod_rows, grad_rows, (((0,), (0,)), ((), ())), preferred_element_type=jnp.float32
        ).astype(jnp.bfloat16),
        "space",
        scatter_dimension=0,
        tiled=True,
    )
    grad_weight = lax.psum(row_share, "frame").astype(jnp.float32) * grad_scale_factor
    grad_hidden = lax.dot_general(
        grad_rows, w_full, (((1,), (1,)), ((), ())), preferred_element_type=jnp.float32
    )
    grad_hidden = grad_hidden.reshape(values_in.shape)
    local_sums = jnp.stack(
        [jnp.sum(grad_hidden, axis=(1, 2, 3)), jnp.sum(grad_hidden * normed, axis=(1, 2, 3))],
        axis=1,
    )
    grad_modulation = lax.psum(local_sums, ("frame", "space")) * grad_scale_factor
    grad_normed = grad_hidden * (1.0 + scale)
    grad_input = (
        grad_normed
        - jnp.mean(grad_normed, axis=-1, keepdims=True)
        - normed * jnp.mean(grad_normed * normed, axis=-1, keepdims=True)
    ) * inverse_std
    return (grad_input.astype(jnp.bfloat16), grad_weight, grad_modulation)


def solution(mesh):
    in_specs = (
        P(None, "frame", "space", None, None),
        P(None, "frame", "space", None, None),
        P("space", None),
        P(),
        P(),
        P(),
        P(),
    )
    out_specs = (P(None, "frame", "space", None, None), P("space", None), P())
    return jax.shard_map(
        per_device, mesh=mesh, in_specs=in_specs, out_specs=out_specs, check_vma=False
    )
```

profile of v0, /device:TPU:2, one launch (start us, length us, event | category | flops | bytes accessed | tf_op | source)
XLA Modules:
  0.0 491.3 jit_solution(7075564899825200032)
XLA Ops:
  7.2 0.7 all-gather.2.cloned.1.call-update
  7.9 0.0 reduce-scatter.5.cloned.1.call-start
  8.0 0.7 compare_select_fusion.1
  8.6 2.9 gather_fusion
  11.6 0.7 compare_select_fusion
  12.3 0.6 gather_fusion.1
  12.9 1.2 multiply_convert_fusion.2
  14.2 0.6 copy.65
  14.8 0.2 convert_reduce_fusion
  15.0 0.3 fusion.18
  15.3 0.3 fusion.12
  15.6 49.8 %all-gather.2.cloned.1.call-done = bf16[1152,3456]{1,0:T(8,128)(2,1)} async-done(((bf16[72,3456]{1,0:T(8,128)(2,1)}), bf16[1152,3456]{1,0:T(8,128)(2,1)}) %all-gather.2.cloned.1.call-update) | async-done | bytes 7962640 | tf_op jit(solution)/shard_map/all_gather | solution.py:48
  65.5 7.1 %convolution_convert_fusion.1 = bf16[256,3456]{1,0:T(8,128)(2,1)} fusion(bf16[256,1152]{1,0:T(8,128)(2,1)S(1)} %bitcast.76, bf16[1152,3456]{1,0:T(8,128)(2,1)} %all-gather.2.cloned.1.call-done), kind=kOutput, calls=%fused_computation.3 | convolution fusion | flops 2039316480 | bytes 10321920 | tf_op jit(solution)/shard_map/dot_general | solution.py:49
  72.6 2.6 copy.63
  75.2 2.0 reshape.124
  77.2 4.6 pad_maximum_fusion
  81.8 4.9 copy.66
  86.7 67.7 %all_to_all.8 = bf16[2,1,128,4,1152]{4,3,1,0,2:T(4,128)(2,1)S(1)} all-to-all(bf16[2,1,128,4,1152]{4,3,1,0,2:T(4,128)(2,1)} %copy.66), channel_id=1, replica_groups=mesh['frame'=16,'space'=16] {'frame'}, dimensions={2} | all-to-all | bytes 4718592 | tf_op jit(solution)/shard_map/all_to_all | solution.py:57
  154.4 8.8 %reshape.148 = bf16[2,16,8,4,16,72]{5,4,3,0,2,1:T(8,128)(2,1)} reshape(bf16[2,1,128,4,1152]{4,3,1,0,2:T(4,128)(2,1)S(1)} %all_to_all.8) | data formatting | bytes 4718592 | tf_op jit(solution)/shard_map/reshape | solution.py:61
  163.2 3.6 fusion.25
  166.8 1.7 fusion.1
  168.5 1.8 multiply_reduce_fusion
  170.2 2.4 fusion.9
  172.7 2.2 fusion.10
  174.9 3.0 fusion.8
  177.9 0.3 copy.73
  178.2 1.5 stack.21
  179.7 0.3 copy.74
  180.0 1.3 stack.22
  181.4 1.5 copy.75
  182.9 1.3 stack.23
  184.2 0.2 pad_maximum_fusion.1
  184.4 0.1 copy.76
  184.6 40.6 %all_to_all.9 = bf16[2,16,8,3,1152]{4,2,0,3,1:T(8,128)(2,1)S(1)} all-to-all(bf16[2,16,8,3,1152]{4,2,0,3,1:T(8,128)(2,1)S(1)} %copy.76), channel_id=1, replica_groups=mesh['frame'=16,'space'=16] {'frame'}, dimensions={1} | all-to-all | bytes 3538944 | tf_op jit(solution)/shard_map/all_to_all | solution.py:66
  225.2 0.9 copy.77
  226.1 0.2 copy.90
  226.4 0.8 copy-done.4
  227.2 5.5 %convolution_convert_fusion = bf16[1152,3456]{1,0:T(8,128)(2,1)} fusion(bf16[256,1152]{1,0:T(8,128)(2,1)S(1)} %bitcast.77, bf16[256,3456]{1,0:T(8,128)(2,1)S(1)} %bitcast.73), kind=kOutput, calls=%fused_computation.2 | convolution fusion | flops 2042413056 | bytes 10321920 | tf_op jit(solution)/shard_map/dot_general | solution.py:71
  232.7 0.0 all-reduce.3.cloned.1.call-start
  232.8 6.5 %fusion.19 = (f32[256]{0:T(256)}, f32[256,1152]{1,0:T(8,128)S(1)}) fusion(f32[2,1152]{1,0:T(2,128)S(1)} %bitcast.80, bf16[256,3456]{1,0:T(8,128)(2,1)S(1)} %bitcast.74, bf16[1152,3456]{1,0:T(8,128)(2,1)} %all-gather.2.cloned.1.call-done), kind=kOutput, calls=%fused_computation.34 | convolution fusion | flops 2039021312 | bytes 10921984 | tf_op jit(solution)/shard_map/dot_general | solution.py:79
  239.3 0.1 reduce_sum.78
  239.4 1.2 fusion.17
  240.6 77.9 %psum.15 = f32[2,2,1152]{2,0,1:T(2,128)S(1)} all-reduce(f32[2,2,1152]{2,0,1:T(2,128)S(1)} %pad_maximum_fusion.2), channel_id=1, replica_groups=mesh['frame'=16,'space'=16] {'frame','space'}, use_global_device_ids=true, to_apply=%region_10.0 | all-reduce | flops 4608 | bytes 36864 | tf_op jit(solution)/shard_map/psum | solution.py:87
  318.6 0.6 copy.80
  319.2 0.1 div.27
  319.3 1.9 fusion.16
  321.2 161.5 %all-reduce.3.cloned.1.call-done = bf16[72,3456]{1,0:T(8,128)(2,1)} async-done(((bf16[72,3456]{1,0:T(8,128)(2,1)}), bf16[72,3456]{1,0:T(8,128)(2,1)}) %all-reduce.3.cloned.1.call-update) | async-done | bytes 497680 | tf_op jit(solution)/shard_map/psum | solution.py:78
  482.7 2.0 convert_multiply_fusion
  (34 shorter events, 0.2 us)
Async XLA Ops:
  7.2 5.1 %copy-start = (f32[1000]{0:T(1024)S(1)}, f32[1000]{0:T(1024)}, u32[]{:S(2)}) copy-start(f32[1000]{0:T(1024)} %param.11) | copy-start | bytes 12004
  7.2 7.6 %copy-start.2 = (bf16[2,1,2,64,1152]{4,3,2,1,0:T(8,128)(2,1)S(1)}, bf16[2,1,2,64,1152]{4,3,2,1,0:T(8,128)(2,1)}, u32[]{:S(2)}) copy-start(bf16[2,1,2,64,1152]{4,3,2,1,0:T(8,128)(2,1)} %param.7) | copy-start | bytes 1769476
  7.2 58.3 %all-gather.2.cloned.1.call-start = ((), (), s32[]{:S(2)}) async-start(), calls=%async_computation.3 | async-start | bytes 8460288 | tf_op jit(solution)/shard_map/all_gather | solution.py:48
  7.9 311.4 %reduce-scatter.5.cloned.1.call-start = ((), (), s32[]{:S(2)}) async-start(), calls=%async_computation.5 | async-start | bytes 8460288
  15.0 224.4 %copy-start.5 = (f32[2,2,64]{2,1,0:T(2,128)}, f32[2,2,64]{2,1,0:T(2,128)S(1)}, u32[]{:S(2)}) copy-start(f32[2,2,64]{2,1,0:T(2,128)S(1)} %broadcast_multiply_fusion.2) | copy-start | bytes 3076
  15.3 50.2 %copy-start.6 = (f32[2,2,64]{2,1,0:T(2,128)}, f32[2,2,64]{2,1,0:T(2,128)S(1)}, u32[]{:S(2)}) copy-start(f32[2,2,64]{2,1,0:T(2,128)S(1)} %add_rsqrt_fusion) | copy-start | bytes 3076
  15.6 49.8 %copy-start.3 = (bf16[2,1,2,64,1152]{4,3,2,1,0:T(8,128)(2,1)}, bf16[2,1,2,64,1152]{4,3,2,1,0:T(8,128)(2,1)S(1)}, u32[]{:S(2)}) copy-start(bf16[2,1,2,64,1152]{4,3,2,1,0:T(8,128)(2,1)S(1)} %fusion.12) | copy-start | bytes 1769476
  226.1 1.1 copy-start.4
  232.7 250.0 %all-reduce.3.cloned.1.call-start = ((), (), s32[]{:S(2)}) async-start(), calls=%async_computation.4 | async-start | bytes 995328 | tf_op jit(solution)/shard_map/psum | solution.py:78
  239.3 79.9 %copy-start.8 = (f32[256]{0:T(256)S(1)}, f32[256]{0:T(256)}, u32[]{:S(2)}) copy-start(f32[256]{0:T(256)} %get-tuple-element.25) | copy-start | bytes 3076
  239.4 79.9 %copy-start.7 = (f32[2,2,64]{2,1,0:T(2,128)S(1)}, f32[2,2,64]{2,1,0:T(2,128)}, u32[]{:S(2)}) copy-start(f32[2,2,64]{2,1,0:T(2,128)} %copy-done.6) | copy-start | bytes 3076
  319.3 165.5 %copy-start.1 = (f32[1000]{0:T(1024)S(1)}, f32[1000]{0:T(1024)}, u32[]{:S(2)}) copy-start(f32[1000]{0:T(1024)} %param.11) | copy-start | bytes 12004
Sparse Core Ops, SparseCore 0:
  9.9 55.5 all-gather.1
  232.9 74.6 reduce-scatter.4
  319.4 163.2 all-reduce.2
where the time goes:
time: 492 us; the launch traced here: 491 us
  waiting for transfers between devices  212 us (43%)
  blocking collectives  186 us (38%)
  local copies, waits for them, and re-layouts  35.1 us (7%)
  matrix products  30.3 us (6%)
  between operations  14 us (3%)
  other arithmetic  13.4 us (3%)
    psum x1, waiting for transfers between devices, per_device(): lax.psum(row_share, 'frame').astype(jnp.float32) * grad_scale_factor  162 us
    psum x1, blocking collectives, per_device(): lax.psum(local_sums, ('frame', 'space')) * grad_scale_factor  77.9 us
    all_to_all x1, blocking collectives, per_device(): lax.all_to_all(packed, 'frame', split_axis=2, concat_axis=1, tiled=True)  67.7 us
    all_gather x1, waiting for transfers between devices, per_device(): w_full = lax.all_gather(w_qkv, 'space', axis=0, tiled=True)  49.8 us
    all_to_all x1, blocking collectives, per_device(): lax.all_to_all(stacked, 'frame', split_axis=1, concat_axis=2, tiled=True)  40.6 us
  transfers between devices with their start and end apart: 3, of which 2 were waited for; matrix products, arithmetic and copies ran while one was open for 4% of the time, Pallas kernels for 0%

commit v1 on v0

--- a/solution.py
+++ b/solution.py
@@ -5,6 +5,12 @@
 
 HEADS = 16
 HEAD_DIM = 72
+
+
+def stacked_exchange(array, axis, split, join):
+    pieces = jnp.split(array, lax.axis_size(axis), axis=split)
+    received = lax.all_to_all(jnp.stack(pieces), axis, 0, 0)
+    return jnp.concatenate(received, axis=join)
 
 
 def attend_back(queries, keys, values, upstream):
@@ -54,7 +60,7 @@
     )
     upstream = upstream.reshape(clip_count, frame_dev, positions, 1, model_width)
     packed = jnp.concatenate([projected, upstream], axis=3)
-    received = lax.all_to_all(packed, "frame", split_axis=2, concat_axis=1, tiled=True)
+    received = stacked_exchange(packed, "frame", 2, 1)
     item_count = received.shape[0]
     frames = received.shape[1]
     across = received.shape[2]

time: 492 us -> 668 us (1.36); the launches traced: 491 us -> 657 us
  local copies, waits for them, and re-layouts: 35.1 us -> 127 us
  other arithmetic: 13.4 us -> 87.7 us
    another operation x0 -> x18, local copies, waits for them, and re-layouts: none -> 96.4 us  [the longest x17 88 us: stacked_exchange(): received = lax.all_to_all(jnp.stack(pieces), axis, 0, 0)]
    another operation x0 -> x4, other arithmetic: none -> 79.6 us  [stacked_exchange(): received = lax.all_to_all(jnp.stack(pieces), axis, 0, 0)]
    reshape x1 -> x0, local copies, waits for them, and re-layouts: 8.77 us -> none  [per_device(): pieces = received.reshape(item_count, frames, across, 4, HEADS, HEAD_DIM)]
    unnamed x22 -> x55, local copies, waits for them, and re-layouts: 1.72 us -> 9.38 us
  transfers between devices with their start and end apart: 3 -> 3, of which waited for: 2 -> 2; matrix products, arithmetic and copies ran while one was open for 4% -> 3% of each run, Pallas kernels for 0% -> 0%
where the time goes in v1:
time: 668 us; the launch traced here: 657 us
  waiting for transfers between devices  212 us (32%)
  blocking collectives  188 us (28%)
  local copies, waits for them, and re-layouts  127 us (19%)
  other arithmetic  87.7 us (13%)
  matrix products  28.4 us (4%)
  between operations  14.6 us (2%)
    psum x1, waiting for transfers between devices, per_device(): lax.psum(row_share, 'frame').astype(jnp.float32) * grad_scale_factor  162 us
    another operation x17, local copies, waits for them, and re-layouts, stacked_exchange(): received = lax.all_to_all(jnp.stack(pieces), axis, 0, 0)  88 us
    another operation x4, other arithmetic, stacked_exchange(): received = lax.all_to_all(jnp.stack(pieces), axis, 0, 0)  79.6 us
    psum x1, blocking collectives, per_device(): lax.psum(local_sums, ('frame', 'space')) * grad_scale_factor  79.4 us
    all_to_all x1, blocking collectives, stacked_exchange(): received = lax.all_to_all(jnp.stack(pieces), axis, 0, 0)  67.5 us
    all_gather x1, waiting for transfers between devices, per_device(): w_full = lax.all_gather(w_qkv, 'space', axis=0, tiled=True)  49.8 us
    all_to_all x1, blocking collectives, per_device(): lax.all_to_all(stacked, 'frame', split_axis=1, concat_axis=2, tiled=True)  40.6 us
  transfers between devices with their start and end apart: 3, of which 2 were waited for; matrix products, arithmetic and copies ran while one was open for 3% of the time, Pallas kernels for 0%

profile of v1, /device:TPU:2, one launch (start us, length us, event | category | flops | bytes accessed | tf_op | source)
XLA Modules:
  0.0 657.4 jit_solution(16833431120377244466)
XLA Ops:
  9.3 2.9 gather_fusion
  12.9 1.2 multiply_convert_fusion.2
  15.6 49.8 %all-gather.2.cloned.1.call-done = bf16[1152,3456]{1,0:T(8,128)(2,1)} async-done(((bf16[72,3456]{1,0:T(8,128)(2,1)}), bf16[1152,3456]{1,0:T(8,128)(2,1)}) %all-gather.2.cloned.1.call-update) | async-done | bytes 7962640 | tf_op jit(solution)/shard_map/all_gather | solution.py:54
  65.4 5.8 convolution_convert_fusion.1
  71.3 2.3 copy.45
  73.6 3.6 reshape.120
  77.2 15.6 %maximum_bitcast_fusion.2 = (bf16[1,2,1,8,4,1152]{3,1,5,4,2,0:T(2,128)(2,1)}, bf16[1,2,1,8,4,1152]{3,1,5,4,2,0:T(2,128)(2,1)}, bf16[1,2,1,8,4,1152]{3,1,5,4,2,0:T(2,128)(2,1)}) fusion(bf16[2,1,128,1,1152]{2,0,4,3,1:T(2,128)(2,1)S(1)} %copy.47, bf16[2,1,128,3,1152]{2,0,4,3,1:T(2,128)(2,1)S(1)} %reshape.120), kind=kLoop, calls=%fused_computation.8 | loop fusion | flops 221184 | bytes 2801664 | tf_op jit(solution)/shard_map/stack | solution.py:12
  92.7 21.2 %maximum_bitcast_fusion.1 = (bf16[1,2,1,8,4,1152]{3,1,5,4,2,0:T(2,128)(2,1)}, bf16[1,2,1,8,4,1152]{3,1,5,4,2,0:T(2,128)(2,1)}, bf16[1,2,1,8,4,1152]{3,1,5,4,2,0:T(2,128)(2,1)}, bf16[1,2,1,8,4,1152]{3,1,5,4,2,0:T(2,128)(2,1)}) fusion(bf16[2,1,128,1,1152]{2,0,4,3,1:T(2,128)(2,1)S(1)} %copy.47, bf16[2,1,128,3,1152]{2,0,4,3,1:T(2,128)(2,1)S(1)} %reshape.120), kind=kLoop, calls=%fused_computation.7 | loop fusion | flops 294912 | bytes 2949120 | tf_op jit(solution)/shard_map/stack | solution.py:12
  114.0 21.2 %maximum_bitcast_fusion = (bf16[1,2,1,8,4,1152]{3,1,5,4,2,0:T(2,128)(2,1)}, bf16[1,2,1,8,4,1152]{3,1,5,4,2,0:T(2,128)(2,1)}, bf16[1,2,1,8,4,1152]{3,1,5,4,2,0:T(2,128)(2,1)}, bf16[1,2,1,8,4,1152]{3,1,5,4,2,0:T(2,128)(2,1)}) fusion(bf16[2,1,128,1,1152]{2,0,4,3,1:T(2,128)(2,1)S(1)} %copy.47, bf16[2,1,128,3,1152]{2,0,4,3,1:T(2,128)(2,1)S(1)} %reshape.120), kind=kLoop, calls=%fused_computation.6 | loop fusion | flops 294912 | bytes 2949120 | tf_op jit(solution)/shard_map/stack | solution.py:12
  135.2 21.5 %fusion = (bf16[1,2,1,8,4,1152]{3,1,5,4,2,0:T(2,128)(2,1)}, bf16[1,2,1,8,4,1152]{3,1,5,4,2,0:T(2,128)(2,1)}, bf16[1,2,1,8,4,1152]{3,1,5,4,2,0:T(2,128)(2,1)}, bf...) fusion(bf16[2,1,128,1,1152]{2,0,4,3,1:T(2,128)(2,1)S(1)} %copy.47, ...), kind=kLoop, calls=%fused_computation.5 | loop fusion | flops 1474560 | bytes 3096576 | tf_op jit(solution)/shard_map/stack | solution.py:12
  156.8 4.8 copy.60
  161.5 4.9 copy.58
  166.5 4.8 copy.59
  171.2 2.0 copy.61
  173.3 6.0 copy.55
  179.2 5.8 copy.56
  185.1 3.8 copy.57
  188.8 5.9 copy.62
  194.8 5.8 copy.52
  200.6 3.7 copy.53
  204.3 6.0 copy.54
  210.3 5.8 copy.63
  216.1 3.8 copy.48
  219.8 6.0 copy.49
  225.8 5.8 copy.50
  231.6 13.3 %copy.51 = bf16[1,2,1,8,4,1152]{5,3,4,2,1,0:T(8,128)(2,1)} copy(bf16[1,2,1,8,4,1152]{3,1,5,4,2,0:T(2,128)(2,1)S(1)} %copy-done.3) | data formatting | bytes 294912 | tf_op jit(solution)/shard_map/stack | solution.py:12
  244.9 1.0 constant_dynamic-update-slice_fusion.15
  245.9 0.9 constant_dynamic-update-slice_fusion.14
  252.7 67.5 %all_to_all.14 = bf16[16,2,1,8,4,1152]{5,3,4,2,1,0:T(8,128)(2,1)S(1)} all-to-all(bf16[16,2,1,8,4,1152]{5,3,4,2,1,0:T(8,128)(2,1)S(1)} %constant_dynamic-update-slice_fusion), channel_id=1, replica_groups=mesh['frame'=16,'space'=16] {'frame'}, dimensions={0} | all-to-all | bytes 4718592 | tf_op jit(solution)/shard_map/all_to_all | solution.py:12
  320.2 8.3 %reshape.144 = bf16[2,16,8,4,16,72]{5,4,2,3,0,1:T(8,128)(2,1)} reshape(bf16[2,16,1,8,4,1152]{5,3,4,2,0,1:T(8,128)(2,1)S(1)} %bitcast.110) | data formatting | bytes 4718592 | tf_op jit(solution)/shard_map/reshape;reshape | solution.py:67
  328.5 3.8 fusion.26
  332.3 1.7 fusion.2
  334.0 2.0 fusion.9
  335.9 1.8 multiply_reduce_fusion
  337.7 3.3 fusion.11
  341.0 2.4 fusion.10
  343.7 1.5 stack.91
  345.5 1.3 stack.89
  346.8 1.5 copy.71
  348.3 1.3 stack.90
  350.0 40.6 %all_to_all.15 = bf16[2,16,8,3,1152]{4,2,0,3,1:T(8,128)(2,1)S(1)} all-to-all(bf16[2,16,8,3,1152]{4,2,0,3,1:T(8,128)(2,1)S(1)} %copy.73), channel_id=1, replica_groups=mesh['frame'=16,'space'=16] {'frame'}, dimensions={1} | all-to-all | bytes 3538944 | tf_op jit(solution)/shard_map/all_to_all | solution.py:72
  392.6 5.5 convolution_convert_fusion
  398.2 5.9 fusion.20
  404.4 1.1 fusion.18
  405.5 79.4 %psum.15 = f32[2,2,1152]{2,0,1:T(2,128)S(1)} all-reduce(f32[2,2,1152]{2,0,1:T(2,128)S(1)} %pad_maximum_fusion.2), channel_id=1, replica_groups=mesh['frame'=16,'space'=16] {'frame','space'}, use_global_device_ids=true, to_apply=%region_10.0 | all-reduce | flops 4608 | bytes 36864 | tf_op jit(solution)/shard_map/psum | solution.py:93
  485.6 1.2 fusion.17
  486.9 161.5 %all-reduce.3.cloned.1.call-done = bf16[72,3456]{1,0:T(8,128)(2,1)} async-done(((bf16[72,3456]{1,0:T(8,128)(2,1)}), bf16[72,3456]{1,0:T(8,128)(2,1)}) %all-reduce.3.cloned.1.call-update) | async-done | bytes 497680 | tf_op jit(solution)/shard_map/psum | solution.py:84
  648.4 2.0 convert_multiply_fusion
  (85 shorter events, 13.8 us)
Async XLA Ops:
  7.2 5.1 copy-start
  7.2 7.6 %copy-start.2 = (bf16[2,1,2,64,1152]{4,3,2,1,0:T(8,128)(2,1)S(1)}, bf16[2,1,2,64,1152]{4,3,2,1,0:T(8,128)(2,1)}, u32[]{:S(2)}) copy-start(bf16[2,1,2,64,1152]{4,3,2,1,0:T(8,128)(2,1)} %param.7) | copy-start | bytes 1769476
  7.2 58.2 %all-gather.2.cloned.1.call-start = ((), (), s32[]{:S(2)}) async-start(), calls=%async_computation.3 | async-start | bytes 8460288 | tf_op jit(solution)/shard_map/all_gather | solution.py:54
  7.9 477.7 %reduce-scatter.5.cloned.1.call-start = ((), (), s32[]{:S(2)}) async-start(), calls=%async_computation.5 | async-start | bytes 8460288
  15.0 56.3 %copy-start.14 = (f32[2,2,64]{2,1,0:T(2,128)}, f32[2,2,64]{2,1,0:T(2,128)S(1)}, u32[]{:S(2)}) copy-start(f32[2,2,64]{2,1,0:T(2,128)S(1)} %broadcast_multiply_fusion.2) | copy-start | bytes 3076
  15.3 50.1 %copy-start.16 = (f32[2,2,64]{2,1,0:T(2,128)}, f32[2,2,64]{2,1,0:T(2,128)S(1)}, u32[]{:S(2)}) copy-start(f32[2,2,64]{2,1,0:T(2,128)S(1)} %add_rsqrt_fusion) | copy-start | bytes 3076
  15.6 55.7 %copy-start.8 = (bf16[2,1,2,64,1152]{4,3,2,1,0:T(8,128)(2,1)}, bf16[2,1,2,64,1152]{4,3,2,1,0:T(8,128)(2,1)S(1)}, u32[]{:S(2)}) copy-start(bf16[2,1,2,64,1152]{4,3,2,1,0:T(8,128)(2,1)S(1)} %fusion.13) | copy-start | bytes 1769476
  161.5 9.7 %copy-start.7 = (bf16[1,2,1,8,4,1152]{3,1,5,4,2,0:T(2,128)(2,1)S(1)}, bf16[1,2,1,8,4,1152]{3,1,5,4,2,0:T(2,128)(2,1)}, u32[]{:S(2)}) copy-start(bf16[1,2,1,8,4,1152]{3,1,5,4,2,0:T(2,128)(2,1)} %get-tuple-element.27) | copy-start | bytes 442372
  173.3 11.8 %copy-start.6 = (bf16[1,2,1,8,4,1152]{3,1,5,4,2,0:T(2,128)(2,1)S(1)}, bf16[1,2,1,8,4,1152]{3,1,5,4,2,0:T(2,128)(2,1)}, u32[]{:S(2)}) copy-start(bf16[1,2,1,8,4,1152]{3,1,5,4,2,0:T(2,128)(2,1)} %get-tuple-element.30) | copy-start | bytes 442372
  188.8 11.7 %copy-start.5 = (bf16[1,2,1,8,4,1152]{3,1,5,4,2,0:T(2,128)(2,1)S(1)}, bf16[1,2,1,8,4,1152]{3,1,5,4,2,0:T(2,128)(2,1)}, u32[]{:S(2)}) copy-start(bf16[1,2,1,8,4,1152]{3,1,5,4,2,0:T(2,128)(2,1)} %get-tuple-element.25) | copy-start | bytes 442372
  204.3 11.8 %copy-start.4 = (bf16[1,2,1,8,4,1152]{3,1,5,4,2,0:T(2,128)(2,1)S(1)}, bf16[1,2,1,8,4,1152]{3,1,5,4,2,0:T(2,128)(2,1)}, u32[]{:S(2)}) copy-start(bf16[1,2,1,8,4,1152]{3,1,5,4,2,0:T(2,128)(2,1)} %get-tuple-element.19) | copy-start | bytes 442372
  219.8 11.8 %copy-start.3 = (bf16[1,2,1,8,4,1152]{3,1,5,4,2,0:T(2,128)(2,1)S(1)}, bf16[1,2,1,8,4,1152]{3,1,5,4,2,0:T(2,128)(2,1)}, u32[]{:S(2)}) copy-start(bf16[1,2,1,8,4,1152]{3,1,5,4,2,0:T(2,128)(2,1)} %get-tuple-element.22) | copy-start | bytes 442372
  244.9 7.5 %copy-start.12 = (bf16[1,2,1,8,4,1152]{5,3,4,2,1,0:T(8,128)(2,1)S(1)}, bf16[1,2,1,8,4,1152]{5,3,4,2,1,0:T(8,128)(2,1)}, u32[]{:S(2)}) copy-start(bf16[1,2,1,8,4,1152]{5,3,4,2,1,0:T(8,128)(2,1)} %copy.56) | copy-start | bytes 442372
  244.9 7.6 %copy-start.13 = (bf16[1,2,1,8,4,1152]{5,3,4,2,1,0:T(8,128)(2,1)S(1)}, bf16[1,2,1,8,4,1152]{5,3,4,2,1,0:T(8,128)(2,1)}, u32[]{:S(2)}) copy-start(bf16[1,2,1,8,4,1152]{5,3,4,2,1,0:T(8,128)(2,1)} %copy.57) | copy-start | bytes 442372
  244.9 7.7 %copy-start.10 = (bf16[1,2,1,8,4,1152]{5,3,4,2,1,0:T(8,128)(2,1)S(1)}, bf16[1,2,1,8,4,1152]{5,3,4,2,1,0:T(8,128)(2,1)}, u32[]{:S(2)}) copy-start(bf16[1,2,1,8,4,1152]{5,3,4,2,1,0:T(8,128)(2,1)} %copy.62) | copy-start | bytes 442372
  244.9 7.7 %copy-start.11 = (bf16[1,2,1,8,4,1152]{5,3,4,2,1,0:T(8,128)(2,1)S(1)}, bf16[1,2,1,8,4,1152]{5,3,4,2,1,0:T(8,128)(2,1)}, u32[]{:S(2)}) copy-start(bf16[1,2,1,8,4,1152]{5,3,4,2,1,0:T(8,128)(2,1)} %copy.63) | copy-start | bytes 442372
  391.6 1.1 copy-start.9
  398.2 250.2 %all-reduce.3.cloned.1.call-start = ((), (), s32[]{:S(2)}) async-start(), calls=%async_computation.4 | async-start | bytes 995328 | tf_op jit(solution)/shard_map/psum | solution.py:84
  404.3 81.3 %copy-start.15 = (f32[2,2,64]{2,1,0:T(2,128)S(1)}, f32[2,2,64]{2,1,0:T(2,128)}, u32[]{:S(2)}) copy-start(f32[2,2,64]{2,1,0:T(2,128)} %copy-done.14) | copy-start | bytes 3076
  404.3 81.3 %copy-start.17 = (f32[2,2,64]{2,1,0:T(2,128)S(1)}, f32[2,2,64]{2,1,0:T(2,128)}, u32[]{:S(2)}) copy-start(f32[2,2,64]{2,1,0:T(2,128)} %copy-done.16) | copy-start | bytes 3076
  404.4 246.1 %copy-start.1 = (f32[1000]{0:T(1024)S(1)}, f32[1000]{0:T(1024)}, u32[]{:S(2)}) copy-start(f32[1000]{0:T(1024)} %param.11) | copy-start | bytes 12004
Sparse Core Ops, SparseCore 0:
  9.9 55.5 all-gather.1
  398.3 74.6 reduce-scatter.4
  485.7 162.6 all-reduce.2
